TPU v7x, 32 devices: a whole 2x2x4 slice. The times are simulated.
32 devices in a mesh: groups: 2 (over x), spatial: 16 (over z, y, core).
Axes of the slice: x: 2, y: 2, z: 4, core: 2. Of those that a mesh axis runs over, the one named last changes fastest.
Arguments:
- fields: bfloat16 [1024, 128, 768], P(('groups', 'spatial')), parts along dimension 0, may hold values from -6 to 6
- norm1_gain: float32 [768], replicated, may hold values from 0.5 to 1.5
- norm1_bias: float32 [768], replicated, may hold values from -3 to 3
- spectral_w1: float32 [2, 8, 96, 96], replicated, may hold values from -0.4375 to 0.4375
- spectral_b1: float32 [2, 8, 96], replicated, may hold values from -3 to 3
- spectral_w2: float32 [2, 8, 96, 96], replicated, may hold values from -0.4375 to 0.4375
- spectral_b2: float32 [2, 8, 96], replicated, may hold values from -3 to 3
- norm2_gain: float32 [768], replicated, may hold values from 0.5 to 1.5
- norm2_bias: float32 [768], replicated, may hold values from -3 to 3
- fc1_weight: bfloat16 [768, 3072], replicated, may hold values from -0.21875 to 0.21875
- fc1_bias: float32 [3072], replicated, may hold values from -3 to 3
- fc2_weight: bfloat16 [3072, 768], replicated, may hold values from -0.109375 to 0.109375
- fc2_bias: float32 [768], replicated, may hold values from -3 to 3
Outputs:
- next_state: bfloat16 [1024, 128, 768], P(('groups', 'spatial')), parts along dimension 0
- anomaly: bfloat16 [1024, 128, 768], P(('groups', 'spatial')), parts along dimension 0
There are 2 independent parts, one for each index of `groups`. A program takes and returns all parts, laid end to end along the dimension named above; an argument that names none is the same for every part. Nothing has to cross between parts.
All inputs are finite; a program needn't handle non-finite values.
Results may differ from a plain program's by a relative error of at most 0.0056.
Values may be sent and summed in bfloat16 or wider, within the bound.
A program may use at most 192 MiB of HBM per device.

v0:
```python
import math

import jax
import jax.numpy as jnp
from jax import lax
from jax.sharding import PartitionSpec as P

MEMBERS = 8


EPSILON = 1e-06
SHRINK = 0.01
FULL_PRECISION = lax.Precision.HIGHEST


def from_behind(block, axis, distance):
    devices = range(lax.axis_size(axis))
    route = [((i - distance) % len(devices), i) for i in devices]
    return lax.ppermute(block, axis, route)


def layer_norm(values, gain, offset_term):
    center = values - jnp.mean(values, axis=-1, keepdims=True)
    spread = jnp.mean(center * center, axis=-1, keepdims=True)
    return center * lax.rsqrt(spread + EPSILON) * gain + offset_term


def soft_shrink(values):
    return jnp.where(
        values > SHRINK, values - SHRINK, jnp.where(values < -SHRINK, values + SHRINK, 0.0)
    )


def contract(form, left, right):
    return jnp.einsum(form, left, right, precision=FULL_PRECISION)


def block_product(values, weight):
    return jnp.einsum("...bi,bio->...bo", values, weight, precision=FULL_PRECISION)


def angle_table(first_len, second_len, modulus):
    first_index = lax.broadcasted_iota(jnp.int32, (first_len, second_len), 0)
    second_index = lax.broadcasted_iota(jnp.int32, (first_len, second_len), 1)
    phase = first_index * second_index % modulus
    return phase.astype(jnp.float32) * (2.0 * math.pi / modulus)


def spectral_layer(real_part, imag_part, w_first, b_first, w_second, b_second):
    shape = real_part.shape
    block_count = w_first.shape[1]
    split_shape = shape[:-1] + (block_count, shape[-1] // block_count)
    real_part = real_part.reshape(split_shape)
    imag_part = imag_part.reshape(split_shape)
    hidden_real = jax.nn.relu(
        block_product(real_part, w_first[0]) - block_product(imag_part, w_first[1]) + b_first[0]
    )
    hidden_imag = jax.nn.relu(
        block_product(imag_part, w_first[0]) + block_product(real_part, w_first[1]) + b_first[1]
    )
    mixed_real = (
        block_product(hidden_real, w_second[0])
        - block_product(hidden_imag, w_second[1])
        + b_second[0]
    )
    mixed_imag = (
        block_product(hidden_imag, w_second[0])
        + block_product(hidden_real, w_second[1])
        + b_second[1]
    )
    return (soft_shrink(mixed_real).reshape(shape), soft_shrink(mixed_imag).reshape(shape))


def longitude_forward(normed, lon_len):
    angles = angle_table(lon_len, lon_len // 2, lon_len)
    factor = 1.0 / math.sqrt(lon_len)
    real_part = contract("rld,lk->rkd", normed, jnp.cos(angles) * factor)
    imag_part = -contract("rld,lk->rkd", normed, jnp.sin(angles) * factor)
    return (real_part, imag_part)


def longitude_inverse(real_part, imag_part, lon_len):
    half_len = lon_len // 2
    angles = angle_table(lon_len, half_len, lon_len)
    column_index = lax.broadcasted_iota(jnp.int32, (1, half_len), 1)
    weights = jnp.where(column_index == 0, 1.0, 2.0) / math.sqrt(lon_len)
    cosine_table = jnp.cos(angles) * weights
    sine_table = jnp.sin(angles) * weights
    return contract("rkd,lk->rld", real_part, cosine_table) - contract(
        "rkd,lk->rld", imag_part, sine_table
    )


def latitude_work(real_part, imag_part, w_first, b_first, w_second, b_second):
    member_rows, mode_count, channels = real_part.shape
    lat_len = member_rows // MEMBERS
    angles = angle_table(lat_len, lat_len, lat_len)
    factor = 1.0 / math.sqrt(lat_len)
    cosine_table = jnp.cos(angles) * factor
    sine_table = jnp.sin(angles) * factor
    grid_real = real_part.reshape(MEMBERS, lat_len, mode_count, channels)
    grid_imag = imag_part.reshape(MEMBERS, lat_len, mode_count, channels)
    spec_real = contract("qp,mpkd->mqkd", cosine_table, grid_real) + contract(
        "qp,mpkd->mqkd", sine_table, grid_imag
    )
    spec_imag = contract("qp,mpkd->mqkd", cosine_table, grid_imag) - contract(
        "qp,mpkd->mqkd", sine_table, grid_real
    )
    mixed_real, mixed_imag = spectral_layer(
        spec_real, spec_imag, w_first, b_first, w_second, b_second
    )
    back_real = contract("qp,mpkd->mqkd", cosine_table, mixed_real) - contract(
        "qp,mpkd->mqkd", sine_table, mixed_imag
    )
    back_imag = contract("qp,mpkd->mqkd", cosine_table, mixed_imag) + contract(
        "qp,mpkd->mqkd", sine_table, mixed_real
    )
    return (
        back_real.reshape(member_rows, mode_count, channels),
        back_imag.reshape(member_rows, mode_count, channels),
    )


def on_device(
    fields,
    norm1_gain,
    norm1_bias,
    spectral_w1,
    spectral_b1,
    spectral_w2,
    spectral_b2,
    norm2_gain,
    norm2_bias,
    fc1_weight,
    fc1_bias,
    fc2_weight,
    fc2_bias,
):
    row_count, lon_len, channels = fields.shape
    state = fields.astype(jnp.float32)
    normed = layer_norm(state, norm1_gain, norm1_bias)
    real_part, imag_part = longitude_forward(normed, lon_len)
    real_part, imag_part = (
        lax.all_to_all(real_part, "spatial", split_axis=1, concat_axis=0, tiled=True),
        lax.all_to_all(imag_part, "spatial", split_axis=1, concat_axis=0, tiled=True),
    )
    real_part, imag_part = latitude_work(
        real_part, imag_part, spectral_w1, spectral_b1, spectral_w2, spectral_b2
    )
    real_part, imag_part = (
        lax.all_to_all(real_part, "spatial", split_axis=0, concat_axis=1, tiled=True),
        lax.all_to_all(imag_part, "spatial", split_axis=0, concat_axis=1, tiled=True),
    )
    filtered = longitude_inverse(real_part, imag_part, lon_len)
    residual = (filtered + normed + state).reshape(row_count * lon_len, channels)
    normed2 = layer_norm(residual, norm2_gain, norm2_bias).astype(jnp.bfloat16)
    hidden = jax.nn.gelu(
        jnp.dot(normed2, fc1_weight, preferred_element_type=jnp.float32) + fc1_bias,
        approximate=False,
    ).astype(jnp.bfloat16)
    updated = residual + jnp.dot(hidden, fc2_weight, preferred_element_type=jnp.float32) + fc2_bias
    next_state = updated.astype(jnp.bfloat16).reshape(row_count, lon_len, channels)
    device_count = lax.axis_size("spatial")
    member_span = device_count // MEMBERS
    state_values = next_state.astype(jnp.float32)

    def advance(counter, state_pair):
        moving, summed = state_pair
        moving = from_behind(moving, "spatial", member_span)
        return (moving, summed + moving.astype(jnp.float32))

    ignored, summed = lax.fori_loop(0, MEMBERS - 1, advance, (next_state, state_values))
    ensemble_mean = summed / MEMBERS
    anomaly = (state_values - ensemble_mean).astype(jnp.bfloat16)
    return (next_state, anomaly)


def solution(mesh):
    placed = (
        P(("groups", "spatial"), None, None),
        P(),
        P(),
        P(),
        P(),
        P(),
        P(),
        P(),
        P(),
        P(),
        P(),
        P(),
        P(),
    )
    return jax.shard_map(
        on_device,
        mesh=mesh,
        in_specs=placed,
        out_specs=(P(("groups", "spatial"), None, None), P(("groups", "spatial"), None, None)),
        check_vma=False,
    )
```

profile of v0, /device:TPU:0, one launch (start us, length us, event | category | flops | bytes accessed | tf_op | source)
XLA Modules:
  0.0 2131.6 jit_solution(12978921306262983575)
XLA Ops:
  7.6 9.6 negate_bitcast_fusion
  31.3 12.0 fusion.94
  49.6 95.7 %all-to-all-done.1 = f32[32,64,768]{2,0,1:T(8,128)} async-done(((f32[32,64,768]{2,0,1:T(8,128)}), f32[32,64,768]{2,0,1:T(8,128)}, u32[]{:S(2)}, u32[]{:S(2)}) %all-to-all-start.1) | async-done | bytes 6291488 | tf_op jit(solution)/shard_map/all_to_all | solution.py:145
  145.3 28.5 %all-to-all-start = ((f32[32,64,768]{2,0,1:T(8,128)}), f32[32,64,768]{2,0,1:T(8,128)}, u32[]{:S(2)}, u32[]{:S(2)}) async-start(f32[32,64,768]{2,0,1:T(8,128)} %copy.55), calls=%async_computation | async-start | bytes 12582912 | tf_op jit(solution)/shard_map/all_to_all | solution.py:144
  193.1 94.8 %all-to-all-done = f32[32,64,768]{2,0,1:T(8,128)} async-done(((f32[32,64,768]{2,0,1:T(8,128)}), f32[32,64,768]{2,0,1:T(8,128)}, u32[]{:S(2)}, u32[]{:S(2)}) %all-to-all-start) | async-done | bytes 6291488 | tf_op jit(solution)/shard_map/all_to_all | solution.py:144
  302.2 9.9 reshape.102
  312.1 13.7 fusion.58
  325.9 9.9 fusion.60
  335.7 8.2 add_bitcast_fusion.1
  343.9 9.9 reshape.101
  353.8 13.1 add_maximum_fusion
  367.0 9.5 fusion.50
  376.4 9.8 fusion.52
  386.3 9.6 add_maximum_fusion.1
  395.9 14.9 select_bitcast_fusion
  410.8 11.0 copy.68
  421.8 9.6 reshape.104
  431.4 12.2 select_bitcast_fusion.1
  443.7 11.0 copy.67
  454.7 9.6 reshape.103
  464.2 8.3 fusion.128
  472.5 8.7 subtract_bitcast_fusion
  488.4 28.3 %all-to-all-start.2 = ((f32[512,4,768]{2,1,0:T(4,128)}), f32[512,4,768]{2,1,0:T(4,128)}, u32[]{:S(2)}, u32[]{:S(2)}) async-start(f32[512,4,768]{2,1,0:T(4,128)} %copy.70), calls=%async_computation.2 | async-start | bytes 12582912 | tf_op jit(solution)/shard_map/all_to_all | solution.py:151
  516.7 8.6 fusion.126
  539.2 91.5 %all-to-all-done.2 = f32[512,4,768]{2,1,0:T(4,128)} async-done(((f32[512,4,768]{2,1,0:T(4,128)}), f32[512,4,768]{2,1,0:T(4,128)}, u32[]{:S(2)}, u32[]{:S(2)}) %all-to-all-start.2) | async-done | bytes 6291488 | tf_op jit(solution)/shard_map/all_to_all | solution.py:151
  630.7 28.5 %all-to-all-start.3 = ((f32[512,4,768]{2,1,0:T(4,128)}), f32[512,4,768]{2,1,0:T(4,128)}, u32[]{:S(2)}, u32[]{:S(2)}) async-start(f32[512,4,768]{2,1,0:T(4,128)} %copy.74), calls=%async_computation.3 | async-start | bytes 12582912 | tf_op jit(solution)/shard_map/all_to_all | solution.py:152
  677.7 95.6 %all-to-all-done.3 = f32[512,4,768]{2,1,0:T(4,128)} async-done(((f32[512,4,768]{2,1,0:T(4,128)}), f32[512,4,768]{2,1,0:T(4,128)}, u32[]{:S(2)}, u32[]{:S(2)}) %all-to-all-start.3) | async-done | bytes 6291488 | tf_op jit(solution)/shard_map/all_to_all | solution.py:152
  792.0 15.1 fusion.134
  807.1 19.1 fusion.262
  830.9 126.4 %fusion.2.clone.6 = bf16[4096,3072]{1,0:T(8,128)(2,1)} fusion(bf16[4096,768]{1,0:T(8,128)(2,1)S(1)} %fusion.47, bf16[768,3072]{1,0:T(8,128)(2,1)} %param.24, f32[3072]{0:T(1024)S(1)} %copy-done.22), kind=kOutput, calls=%fused_computation.4.clone.clone.clone.clone.clone.1 | convolution fusion | flops 20157825024 | bytes 36188160 | tf_op jit(solution)/shard_map/dot_general | solution.py:158
  957.2 26.3 %fusion.49 = bf16[4096,768]{1,0:T(8,128)(2,1)S(1)} fusion(f32[32,128,768]{2,1,0:T(8,128)} %copy-done, bf16[3072,768]{1,0:T(8,128)(2,1)} %param.26, f32[768]{0:T(1024)S(1)} %copy-done.23, bf16[4096,3072]{1,0:T(8,128)(2,1)} %fusion.2.clone.6), kind=kOutput, calls=%fused_computation.62 | convolution fusion | flops 19336790016 | bytes 48761856 | tf_op jit(solution)/shard_map/dot_general | solution.py:161
  992.4 1127.6 %while.12 = (s32[]{:T(128)}, bf16[32,128,768]{2,1,0:T(8,128)(2,1)}, f32[32,128,768]{2,1,0:T(8,128)}, s32[]{:T(128)}) while((s32[]{:T(128)}, bf16[32,128,768]{2,1,0:T(8,128)(2,1)}, f32[32,128,768]{2,1,0:T(8,128)}, s32[]{:T(128)}) %tuple.26), condition=%wide.region_5.6_spmd, body=%wide.region_4.5_spmd.sunk | while | flops 6291458 | bytes 69206104 | solution.py:172
  992.6 9.1 collective-permute-start
  1001.7 154.1 %collective-permute-done = bf16[32,128,768]{2,1,0:T(8,128)(2,1)} collective-permute-done((bf16[32,128,768]{2,1,0:T(8,128)(2,1)}, bf16[32,128,768]{2,1,0:T(8,128)(2,1)}, u32[]{:S(2)}, u32[]{:S(2)}) %collective-permute-start) | collective-permute-done | bytes 6291488 | tf_op jit(solution)/shard_map/while/body/eval_jaxpr/ppermute | solution.py:19
  1161.9 13.2 convert_add_fusion.3
  1175.1 140.2 %collective-permute-done = bf16[32,128,768]{2,1,0:T(8,128)(2,1)} collective-permute-done((bf16[32,128,768]{2,1,0:T(8,128)(2,1)}, bf16[32,128,768]{2,1,0:T(8,128)(2,1)}, u32[]{:S(2)}, u32[]{:S(2)}) %collective-permute-start) | collective-permute-done | bytes 6291488 | tf_op jit(solution)/shard_map/while/body/eval_jaxpr/ppermute | solution.py:19
  1321.5 13.2 convert_add_fusion.3
  1334.7 139.4 %collective-permute-done = bf16[32,128,768]{2,1,0:T(8,128)(2,1)} collective-permute-done((bf16[32,128,768]{2,1,0:T(8,128)(2,1)}, bf16[32,128,768]{2,1,0:T(8,128)(2,1)}, u32[]{:S(2)}, u32[]{:S(2)}) %collective-permute-start) | collective-permute-done | bytes 6291488 | tf_op jit(solution)/shard_map/while/body/eval_jaxpr/ppermute | solution.py:19
  1480.3 13.2 convert_add_fusion.3
  1493.5 138.5 %collective-permute-done = bf16[32,128,768]{2,1,0:T(8,128)(2,1)} collective-permute-done((bf16[32,128,768]{2,1,0:T(8,128)(2,1)}, bf16[32,128,768]{2,1,0:T(8,128)(2,1)}, u32[]{:S(2)}, u32[]{:S(2)}) %collective-permute-start) | collective-permute-done | bytes 6291488 | tf_op jit(solution)/shard_map/while/body/eval_jaxpr/ppermute | solution.py:19
  1638.2 13.2 convert_add_fusion.3
  1651.4 137.7 %collective-permute-done = bf16[32,128,768]{2,1,0:T(8,128)(2,1)} collective-permute-done((bf16[32,128,768]{2,1,0:T(8,128)(2,1)}, bf16[32,128,768]{2,1,0:T(8,128)(2,1)}, u32[]{:S(2)}, u32[]{:S(2)}) %collective-permute-start) | collective-permute-done | bytes 6291488 | tf_op jit(solution)/shard_map/while/body/eval_jaxpr/ppermute | solution.py:19
  1795.2 13.2 convert_add_fusion.3
  1808.4 136.8 %collective-permute-done = bf16[32,128,768]{2,1,0:T(8,128)(2,1)} collective-permute-done((bf16[32,128,768]{2,1,0:T(8,128)(2,1)}, bf16[32,128,768]{2,1,0:T(8,128)(2,1)}, u32[]{:S(2)}, u32[]{:S(2)}) %collective-permute-start) | collective-permute-done | bytes 6291488 | tf_op jit(solution)/shard_map/while/body/eval_jaxpr/ppermute | solution.py:19
  1951.4 13.2 convert_add_fusion.3
  1964.6 136.0 %collective-permute-done = bf16[32,128,768]{2,1,0:T(8,128)(2,1)} collective-permute-done((bf16[32,128,768]{2,1,0:T(8,128)(2,1)}, bf16[32,128,768]{2,1,0:T(8,128)(2,1)}, u32[]{:S(2)}, u32[]{:S(2)}) %collective-permute-start) | collective-permute-done | bytes 6291488 | tf_op jit(solution)/shard_map/while/body/eval_jaxpr/ppermute | solution.py:19
  2106.7 13.2 convert_add_fusion.3
  2120.0 11.2 subtract_convert_fusion
  (123 shorter events, 175.3 us)
Async XLA Ops:
  0.6 4.6 copy-start.3
  0.6 7.0 copy-start.16
  0.7 7.0 copy-start.18
  5.2 26.0 %copy-start.10 = (f32[32,128]{1,0:T(8,128)}, f32[32,128]{1,0:T(8,128)S(1)}, u32[]{:S(2)}) copy-start(f32[32,128]{1,0:T(8,128)S(1)} %broadcast_multiply_fusion.1) | copy-start | bytes 49156
  7.6 23.6 %copy-start.12 = (f32[32,128]{1,0:T(8,128)}, f32[32,128]{1,0:T(8,128)S(1)}, u32[]{:S(2)}) copy-start(f32[32,128]{1,0:T(8,128)S(1)} %add_rsqrt_fusion) | copy-start | bytes 49156
  23.8 121.5 %all-to-all-start.1 = ((f32[32,64,768]{2,0,1:T(8,128)}), f32[32,64,768]{2,0,1:T(8,128)}, u32[]{:S(2)}, u32[]{:S(2)}) async-start(f32[32,64,768]{2,0,1:T(8,128)} %copy.58), calls=%async_computation.1 | async-start | bytes 12582912 | tf_op jit(solution)/shard_map/all_to_all | solution.py:145
  49.6 124.2 %copy-start.14 = (f32[2,8,96]{2,1,0:T(8,128)S(1)}, f32[2,8,96]{2,1,0:T(8,128)}, u32[]{:S(2)}) copy-start(f32[2,8,96]{2,1,0:T(8,128)} %param.19) | copy-start | bytes 18436
  49.6 124.3 %copy-start.15 = (f32[2,8,96]{2,1,0:T(8,128)S(1)}, f32[2,8,96]{2,1,0:T(8,128)}, u32[]{:S(2)}) copy-start(f32[2,8,96]{2,1,0:T(8,128)} %param.21) | copy-start | bytes 18436
  145.3 142.6 %all-to-all-start = ((f32[32,64,768]{2,0,1:T(8,128)}), f32[32,64,768]{2,0,1:T(8,128)}, u32[]{:S(2)}, u32[]{:S(2)}) async-start(f32[32,64,768]{2,0,1:T(8,128)} %copy.55), calls=%async_computation | async-start | bytes 12582912 | tf_op jit(solution)/shard_map/all_to_all | solution.py:144
  193.1 101.2 %slice-start.10 = ((s8[6291456]{0:T(1024)(128)(4,1)}), s8[2097152]{0:T(1024)(128)(4,1)S(1)}, s32[]{:S(2)}) async-start(s8[6291456]{0:T(1024)(128)(4,1)} %bitcast.204), calls=%async_computation.14 | async-start | bytes 4194304
  287.9 6.4 slice-start.11
  291.6 2.7 copy-start.5
  302.2 9.9 copy-start.6
  312.1 13.7 copy-start.1
  312.1 23.6 %slice-start.4 = ((s8[6291456]{0:T(1024)(128)(4,1)}), s8[4194304]{0:T(1024)(128)(4,1)S(1)}, s32[]{:S(2)}) async-start(s8[6291456]{0:T(1024)(128)(4,1)} %bitcast.193), calls=%async_computation.8 | async-start | bytes 8388608
  312.1 23.6 %slice-start.8 = ((s8[6291456]{0:T(1024)(128)(4,1)}), s8[4194304]{0:T(1024)(128)(4,1)S(1)}, s32[]{:S(2)}) async-start(s8[6291456]{0:T(1024)(128)(4,1)} %bitcast.202), calls=%async_computation.12 | async-start | bytes 8388608
  325.8 9.9 slice-start.5
  325.9 9.9 slice-start.9
  353.8 13.2 copy-start.7
  366.9 9.5 copy-start.8
  366.9 19.3 slice-start
  367.0 19.3 slice-start.6
  376.4 9.9 slice-start.1
  376.4 9.9 slice-start.7
  395.9 14.9 copy-start.2
  421.8 9.6 copy-start.9
  488.4 36.9 %slice-start.2 = ((s8[6291456]{0:T(1024)(128)(4,1)}), s8[2097152]{0:T(1024)(128)(4,1)S(1)}, s32[]{:S(2)}) async-start(s8[6291456]{0:T(1024)(128)(4,1)} %bitcast.184), calls=%async_computation.6 | async-start | bytes 4194304
  488.4 142.3 %all-to-all-start.2 = ((f32[512,4,768]{2,1,0:T(4,128)}), f32[512,4,768]{2,1,0:T(4,128)}, u32[]{:S(2)}, u32[]{:S(2)}) async-start(f32[512,4,768]{2,1,0:T(4,128)} %copy.70), calls=%async_computation.2 | async-start | bytes 12582912 | tf_op jit(solution)/shard_map/all_to_all | solution.py:151
  516.7 8.6 slice-start.3
  630.7 142.6 %all-to-all-start.3 = ((f32[512,4,768]{2,1,0:T(4,128)}), f32[512,4,768]{2,1,0:T(4,128)}, u32[]{:S(2)}, u32[]{:S(2)}) async-start(f32[512,4,768]{2,1,0:T(4,128)} %copy.74), calls=%async_computation.3 | async-start | bytes 12582912 | tf_op jit(solution)/shard_map/all_to_all | solution.py:152
  792.0 15.2 copy-start.11
  792.0 15.2 copy-start.13
  792.0 15.2 copy-start.17
  792.0 15.2 copy-start.19
  826.3 4.6 copy-start
  826.3 1.5 copy-start.20
  826.3 1.5 copy-start.21
  827.8 3.1 copy-start.22
  830.9 126.4 %copy-start.23 = (f32[768]{0:T(1024)S(1)}, f32[768]{0:T(1024)}, u32[]{:S(2)}) copy-start(f32[768]{0:T(1024)} %param.27) | copy-start | bytes 9220
  983.5 8.9 copy-start.4
  992.6 163.1 %collective-permute-start = (bf16[32,128,768]{2,1,0:T(8,128)(2,1)}, bf16[32,128,768]{2,1,0:T(8,128)(2,1)}, u32[]{:S(2)}, u32[]{:S(2)}) collective-permute-start(bf16[32,128,768]{2,1,0:T(8,128)(2,1)} %get-tuple-element.58), channel_id=1, source_target_pairs={{14,0},{15,1},{0,2},{1,3},{2,4},{3,5},{4,6},{5,7},{6,8},{7,9},{8,1... | collective-permute-start | bytes 18874376 | tf_op jit(solution)/shard_map/while/body/eval_jaxpr/ppermute | solution.py:19
  1175.1 140.2 %collective-permute-start = (bf16[32,128,768]{2,1,0:T(8,128)(2,1)}, bf16[32,128,768]{2,1,0:T(8,128)(2,1)}, u32[]{:S(2)}, u32[]{:S(2)}) collective-permute-start(bf16[32,128,768]{2,1,0:T(8,128)(2,1)} %get-tuple-element.58), channel_id=1, source_target_pairs={{14,0},{15,1},{0,2},{1,3},{2,4},{3,5},{4,6},{5,7},{6,8},{7,9},{8,1... | collective-permute-start | bytes 18874376 | tf_op jit(solution)/shard_map/while/body/eval_jaxpr/ppermute | solution.py:19
  1334.7 139.4 %collective-permute-start = (bf16[32,128,768]{2,1,0:T(8,128)(2,1)}, bf16[32,128,768]{2,1,0:T(8,128)(2,1)}, u32[]{:S(2)}, u32[]{:S(2)}) collective-permute-start(bf16[32,128,768]{2,1,0:T(8,128)(2,1)} %get-tuple-element.58), channel_id=1, source_target_pairs={{14,0},{15,1},{0,2},{1,3},{2,4},{3,5},{4,6},{5,7},{6,8},{7,9},{8,1... | collective-permute-start | bytes 18874376 | tf_op jit(solution)/shard_map/while/body/eval_jaxpr/ppermute | solution.py:19
  1493.5 138.5 %collective-permute-start = (bf16[32,128,768]{2,1,0:T(8,128)(2,1)}, bf16[32,128,768]{2,1,0:T(8,128)(2,1)}, u32[]{:S(2)}, u32[]{:S(2)}) collective-permute-start(bf16[32,128,768]{2,1,0:T(8,128)(2,1)} %get-tuple-element.58), channel_id=1, source_target_pairs={{14,0},{15,1},{0,2},{1,3},{2,4},{3,5},{4,6},{5,7},{6,8},{7,9},{8,1... | collective-permute-start | bytes 18874376 | tf_op jit(solution)/shard_map/while/body/eval_jaxpr/ppermute | solution.py:19
  1651.4 137.7 %collective-permute-start = (bf16[32,128,768]{2,1,0:T(8,128)(2,1)}, bf16[32,128,768]{2,1,0:T(8,128)(2,1)}, u32[]{:S(2)}, u32[]{:S(2)}) collective-permute-start(bf16[32,128,768]{2,1,0:T(8,128)(2,1)} %get-tuple-element.58), channel_id=1, source_target_pairs={{14,0},{15,1},{0,2},{1,3},{2,4},{3,5},{4,6},{5,7},{6,8},{7,9},{8,1... | collective-permute-start | bytes 18874376 | tf_op jit(solution)/shard_map/while/body/eval_jaxpr/ppermute | solution.py:19
  1808.4 136.8 %collective-permute-start = (bf16[32,128,768]{2,1,0:T(8,128)(2,1)}, bf16[32,128,768]{2,1,0:T(8,128)(2,1)}, u32[]{:S(2)}, u32[]{:S(2)}) collective-permute-start(bf16[32,128,768]{2,1,0:T(8,128)(2,1)} %get-tuple-element.58), channel_id=1, source_target_pairs={{14,0},{15,1},{0,2},{1,3},{2,4},{3,5},{4,6},{5,7},{6,8},{7,9},{8,1... | collective-permute-start | bytes 18874376 | tf_op jit(solution)/shard_map/while/body/eval_jaxpr/ppermute | solution.py:19
  1964.6 136.0 %collective-permute-start = (bf16[32,128,768]{2,1,0:T(8,128)(2,1)}, bf16[32,128,768]{2,1,0:T(8,128)(2,1)}, u32[]{:S(2)}, u32[]{:S(2)}) collective-permute-start(bf16[32,128,768]{2,1,0:T(8,128)(2,1)} %get-tuple-element.58), channel_id=1, source_target_pairs={{14,0},{15,1},{0,2},{1,3},{2,4},{3,5},{4,6},{5,7},{6,8},{7,9},{8,1... | collective-permute-start | bytes 18874376 | tf_op jit(solution)/shard_map/while/body/eval_jaxpr/ppermute | solution.py:19
where the time goes:
time: 2140 us; the launch traced here: 2130 us
  waiting for transfers between devices  1360 us (64%)
  matrix products  365 us (17%)
  local copies, waits for them, and re-layouts  182 us (9%)
  other arithmetic  120 us (6%)
  starting transfers between devices  102 us (5%)
    ppermute x7, waiting for transfers between devices, from_behind(): return lax.ppermute(block, axis, route)  983 us
    dot_general x1, matrix products, on_device(): jnp.dot(normed2, fc1_weight, preferred_element_type=jnp.float32) + fc1_bias  126 us
    dot_general x12, matrix products, contract(): return jnp.einsum(form, left, right, precision=FULL_PRECISION)  120 us
    all_to_all x1, waiting for transfers between devices, on_device(): lax.all_to_all(imag_part, 'spatial', split_axis=1, concat_axis=0, tiled=T...  95.7 us
    all_to_all x1, waiting for transfers between devices, on_device(): lax.all_to_all(imag_part, 'spatial', split_axis=0, concat_axis=1, tiled=T...  95.6 us
    all_to_all x1, waiting for transfers between devices, on_device(): lax.all_to_all(real_part, 'spatial', split_axis=1, concat_axis=0, tiled=T...  94.8 us
    dot_general x8, matrix products, block_product(): jnp.einsum('...bi,bio->...bo', values, weight, precision=FULL_PRECISION)  92.7 us
    add x7, other arithmetic, advance(): return (moving, summed + moving.astype(jnp.float32))  92.6 us
  transfers between devices with their start and end apart: 11, of which 11 were waited for; matrix products, arithmetic and copies ran while one was open for 3% of the time, Pallas kernels for 0%

commit v1 on v0

--- a/solution.py
+++ b/solution.py
@@ -3,7 +3,7 @@
 import jax
 import jax.numpy as jnp
 from jax import lax
-from jax.sharding import PartitionSpec as P
+from jax.sharding import Mesh, PartitionSpec as P
 
 MEMBERS = 8
 
@@ -160,18 +160,13 @@
     ).astype(jnp.bfloat16)
     updated = residual + jnp.dot(hidden, fc2_weight, preferred_element_type=jnp.float32) + fc2_bias
     next_state = updated.astype(jnp.bfloat16).reshape(row_count, lon_len, channels)
-    device_count = lax.axis_size("spatial")
-    member_span = device_count // MEMBERS
+    return next_state
+
+
+def ensemble_step(next_state):
     state_values = next_state.astype(jnp.float32)
-
-    def advance(counter, state_pair):
-        moving, summed = state_pair
-        moving = from_behind(moving, "spatial", member_span)
-        return (moving, summed + moving.astype(jnp.float32))
-
-    ignored, summed = lax.fori_loop(0, MEMBERS - 1, advance, (next_state, state_values))
-    ensemble_mean = summed / MEMBERS
-    anomaly = (state_values - ensemble_mean).astype(jnp.bfloat16)
+    summed = lax.psum(state_values, "member")
+    anomaly = (state_values - summed / MEMBERS).astype(jnp.bfloat16)
     return (next_state, anomaly)
 
 
@@ -191,10 +186,28 @@
         P(),
         P(),
     )
-    return jax.shard_map(
+    update = jax.shard_map(
         on_device,
         mesh=mesh,
         in_specs=placed,
-        out_specs=(P(("groups", "spatial"), None, None), P(("groups", "spatial"), None, None)),
+        out_specs=P(("groups", "spatial"), None, None),
         check_vma=False,
     )
+    member_span = mesh.shape["spatial"] // MEMBERS
+    ensemble_mesh = Mesh(
+        mesh.devices.reshape(mesh.shape["groups"], MEMBERS, member_span),
+        ("groups", "member", "half"),
+    )
+    member_rows = P(("groups", "member", "half"), None, None)
+    spread = jax.shard_map(
+        ensemble_step,
+        mesh=ensemble_mesh,
+        in_specs=(member_rows,),
+        out_specs=(member_rows, member_rows),
+        check_vma=False,
+    )
+
+    def step(*args):
+        return spread(update(*args))
+
+    return step

time: 2140 us -> 1520 us (0.71)
  waiting for transfers between devices: 1360 us -> 378 us
  blocking collectives: 0 us -> 510 us
  other arithmetic: 120 us -> 21.4 us
  local copies, waits for them, and re-layouts: 182 us -> 136 us
    ppermute x7 -> x0, waiting for transfers between devices: 983 us -> none  [from_behind(): return lax.ppermute(block, axis, route)]
    psum x0 -> x1, blocking collectives: none -> 510 us  [ensemble_step(): summed = lax.psum(state_values, 'member')]
    add x7 -> x0, other arithmetic: 92.6 us -> none  [advance(): return (moving, summed + moving.astype(jnp.float32))]
    while x7 -> x0, local copies, waits for them, and re-layouts: 43 us -> none
  transfers between devices with their start and end apart: 11 -> 4, of which waited for: 11 -> 4; matrix products, arithmetic and copies ran while one was open for 3% -> 5% of each run, Pallas kernels for 0% -> 0%
where the time goes in v1:
time: 1520 us; the launch traced here: 1510 us
  blocking collectives  510 us (34%)
  waiting for transfers between devices  378 us (25%)
  matrix products  367 us (24%)
  local copies, waits for them, and re-layouts  136 us (9%)
  starting transfers between devices  92.8 us (6%)
  other arithmetic  21.4 us (1%)
    psum x1, blocking collectives, ensemble_step(): summed = lax.psum(state_values, 'member')  510 us
    dot_general x1, matrix products, on_device(): jnp.dot(normed2, fc1_weight, preferred_element_type=jnp.float32) + fc1_bias  126 us
    dot_general x12, matrix products, contract(): return jnp.einsum(form, left, right, precision=FULL_PRECISION)  120 us
    all_to_all x1, waiting for transfers between devices, on_device(): lax.all_to_all(imag_part, 'spatial', split_axis=1, concat_axis=0, tiled=T...  95.7 us
    all_to_all x1, waiting for transfers between devices, on_device(): lax.all_to_all(imag_part, 'spatial', split_axis=0, concat_axis=1, tiled=T...  95.6 us
    all_to_all x1, waiting for transfers between devices, on_device(): lax.all_to_all(real_part, 'spatial', split_axis=1, concat_axis=0, tiled=T...  94.8 us
    dot_general x8, matrix products, block_product(): jnp.einsum('...bi,bio->...bo', values, weight, precision=FULL_PRECISION)  92.8 us
    all_to_all x1, waiting for transfers between devices, on_device(): lax.all_to_all(real_part, 'spatial', split_axis=0, concat_axis=1, tiled=T...  91.6 us
  transfers between devices with their start and end apart: 4, of which 4 were waited for; matrix products, arithmetic and copies ran while one was open for 5% of the time, Pallas kernels for 0%

profile of v1, /device:TPU:0, one launch (start us, length us, event | category | flops | bytes accessed | tf_op | source)
XLA Modules:
  0.0 1506.0 jit_solution(8603126026089970054)
XLA Ops:
  7.6 9.6 negate_bitcast_fusion
  17.2 6.6 copy.60
  23.8 7.5 all-to-all-start.1
  31.3 12.0 fusion.94
  43.3 6.3 copy.57
  49.6 95.7 %all-to-all-done.1 = f32[32,64,768]{2,0,1:T(8,128)} async-done(((f32[32,64,768]{2,0,1:T(8,128)}), f32[32,64,768]{2,0,1:T(8,128)}, u32[]{:S(2)}, u32[]{:S(2)}) %all-to-all-start.1) | async-done | bytes 6291488 | tf_op jit(solution)/shard_map/all_to_all | solution.py:145
  145.3 28.5 %all-to-all-start = ((f32[32,64,768]{2,0,1:T(8,128)}), f32[32,64,768]{2,0,1:T(8,128)}, u32[]{:S(2)}, u32[]{:S(2)}) async-start(f32[32,64,768]{2,0,1:T(8,128)} %copy.57), calls=%async_computation | async-start | bytes 12582912 | tf_op jit(solution)/shard_map/all_to_all | solution.py:144
  177.4 7.9 fusion.74
  185.3 7.8 fusion.76
  193.1 94.8 %all-to-all-done = f32[32,64,768]{2,0,1:T(8,128)} async-done(((f32[32,64,768]{2,0,1:T(8,128)}), f32[32,64,768]{2,0,1:T(8,128)}, u32[]{:S(2)}, u32[]{:S(2)}) %all-to-all-start) | async-done | bytes 6291488 | tf_op jit(solution)/shard_map/all_to_all | solution.py:144
  294.3 7.9 subtract_bitcast_fusion.1
  302.2 9.9 reshape.102
  312.1 13.7 fusion.58
  325.9 9.9 fusion.60
  335.8 8.2 add_bitcast_fusion.1
  343.9 9.9 reshape.101
  353.8 13.1 add_maximum_fusion
  367.0 9.5 fusion.50
  376.5 9.9 fusion.52
  386.4 9.6 add_maximum_fusion.1
  396.0 14.9 select_bitcast_fusion
  410.9 10.9 copy.70
  421.9 9.6 reshape.104
  431.5 12.2 select_bitcast_fusion.1
  443.7 10.9 copy.69
  454.7 9.6 reshape.103
  464.2 8.3 fusion.128
  472.5 8.7 subtract_bitcast_fusion
  481.8 6.7 copy.72
  488.4 28.2 %all-to-all-start.2 = ((f32[512,4,768]{2,1,0:T(4,128)}), f32[512,4,768]{2,1,0:T(4,128)}, u32[]{:S(2)}, u32[]{:S(2)}) async-start(f32[512,4,768]{2,1,0:T(4,128)} %copy.72), calls=%async_computation.2 | async-start | bytes 12582912 | tf_op jit(solution)/shard_map/all_to_all | solution.py:151
  516.7 8.6 fusion.126
  525.3 6.7 add_bitcast_fusion
  532.5 6.7 copy.76
  539.2 91.6 %all-to-all-done.2 = f32[512,4,768]{2,1,0:T(4,128)} async-done(((f32[512,4,768]{2,1,0:T(4,128)}), f32[512,4,768]{2,1,0:T(4,128)}, u32[]{:S(2)}, u32[]{:S(2)}) %all-to-all-start.2) | async-done | bytes 6291488 | tf_op jit(solution)/shard_map/all_to_all | solution.py:151
  630.7 28.5 %all-to-all-start.3 = ((f32[512,4,768]{2,1,0:T(4,128)}), f32[512,4,768]{2,1,0:T(4,128)}, u32[]{:S(2)}, u32[]{:S(2)}) async-start(f32[512,4,768]{2,1,0:T(4,128)} %copy.76), calls=%async_computation.3 | async-start | bytes 12582912 | tf_op jit(solution)/shard_map/all_to_all | solution.py:152
  659.3 4.0 copy.73
  663.3 6.7 copy.74
  670.0 7.7 all_to_all.57
  677.7 95.6 %all-to-all-done.3 = f32[512,4,768]{2,1,0:T(4,128)} async-done(((f32[512,4,768]{2,1,0:T(4,128)}), f32[512,4,768]{2,1,0:T(4,128)}, u32[]{:S(2)}, u32[]{:S(2)}) %all-to-all-start.3) | async-done | bytes 6291488 | tf_op jit(solution)/shard_map/all_to_all | solution.py:152
  773.3 4.0 copy.77
  777.3 6.7 copy.78
  784.1 7.9 all_to_all.61
  792.0 15.1 %fusion.134 = f32[128,32,768]{2,0,1:T(8,128)} fusion(f32[32,64,768]{2,1,0:T(8,128)} %all_to_all.57, f32[64]{0:T(128)S(1)} %fusion.172), kind=kOutput, calls=%fused_computation.149 | convolution fusion | flops 2416041984 | bytes 18874624 | tf_op jit(solution)/shard_map/rkd,lk->rld/dot_general | solution.py:35
  807.1 19.1 %fusion.262 = (f32[32,128]{1,0:T(8,128)S(1)}, f32[32,128,768]{2,1,0:T(8,128)S(1)}) fusion(f32[768]{0:T(1024)S(1)} %copy-done.16, f32[768]{0:T(1024)S(1)} %copy-done.18, f32[32,128]{1,0:T(8,128)S(1)} %copy-done.12, f32[32,128]{1,0:T(8,128)S(1)} %copy-done.10, bf16[32,128,768]{2,1,0:T(8,128)(2,1)} %param.14, f32[128,32,768]{2,0,1:T(8,128)} %fusion.134, ...), kind=kOutput, calls=%fused_computation.276 | convolution fusion | flops 2444349440 | bytes 37804288 | tf_op jit(solution)/shard_map/rkd,lk->rld/dot_general | solution.py:35
  830.8 126.3 %fusion.2.clone.6 = bf16[4096,3072]{1,0:T(8,128)(2,1)} fusion(bf16[4096,768]{1,0:T(8,128)(2,1)S(1)} %fusion.47, bf16[768,3072]{1,0:T(8,128)(2,1)} %param.23, f32[3072]{0:T(1024)S(1)} %copy-done.21), kind=kOutput, calls=%fused_computation.3.clone.clone.clone.clone.clone.1 | convolution fusion | flops 20157825024 | bytes 36188160 | tf_op jit(solution)/shard_map/dot_general | solution.py:158
  957.2 27.6 %fusion.49 = bf16[4096,768]{1,0:T(8,128)(2,1)} fusion(f32[32,128,768]{2,1,0:T(8,128)} %copy-done, bf16[3072,768]{1,0:T(8,128)(2,1)} %param.25, f32[768]{0:T(1024)S(1)} %copy-done.22, bf16[4096,3072]{1,0:T(8,128)(2,1)} %fusion.2.clone.6), kind=kOutput, calls=%fused_computation.61 | convolution fusion | flops 19336790016 | bytes 48761856 | tf_op jit(solution)/shard_map/dot_general | solution.py:161
  984.7 509.6 %all-reduce.1 = f32[32,128,768]{2,1,0:T(8,128)} all-reduce(bf16[32,128,768]{2,1,0:T(8,128)(2,1)} %bitcast.202), channel_id=1, replica_groups=mesh['groups'=2,'member'=8,'half'=2] {'member'}, use_global_device_ids=true, to_apply=%region_4.6 | all-reduce | flops 3145728 | bytes 18874368 | tf_op jit(solution)/shard_map/psum | solution.py:168
  1494.3 11.2 subtract_convert_fusion
  (91 shorter events, 22.4 us)
Async XLA Ops:
  0.6 4.6 copy-start.3
  0.6 7.0 copy-start.15
  0.7 7.0 copy-start.17
  5.2 26.0 %copy-start.9 = (f32[32,128]{1,0:T(8,128)}, f32[32,128]{1,0:T(8,128)S(1)}, u32[]{:S(2)}) copy-start(f32[32,128]{1,0:T(8,128)S(1)} %broadcast_multiply_fusion.1) | copy-start | bytes 49156
  7.6 23.6 %copy-start.11 = (f32[32,128]{1,0:T(8,128)}, f32[32,128]{1,0:T(8,128)S(1)}, u32[]{:S(2)}) copy-start(f32[32,128]{1,0:T(8,128)S(1)} %add_rsqrt_fusion) | copy-start | bytes 49156
  23.8 121.5 %all-to-all-start.1 = ((f32[32,64,768]{2,0,1:T(8,128)}), f32[32,64,768]{2,0,1:T(8,128)}, u32[]{:S(2)}, u32[]{:S(2)}) async-start(f32[32,64,768]{2,0,1:T(8,128)} %copy.60), calls=%async_computation.1 | async-start | bytes 12582912 | tf_op jit(solution)/shard_map/all_to_all | solution.py:145
  49.6 124.2 %copy-start.13 = (f32[2,8,96]{2,1,0:T(8,128)S(1)}, f32[2,8,96]{2,1,0:T(8,128)}, u32[]{:S(2)}) copy-start(f32[2,8,96]{2,1,0:T(8,128)} %param.18) | copy-start | bytes 18436
  49.6 124.3 %copy-start.14 = (f32[2,8,96]{2,1,0:T(8,128)S(1)}, f32[2,8,96]{2,1,0:T(8,128)}, u32[]{:S(2)}) copy-start(f32[2,8,96]{2,1,0:T(8,128)} %param.20) | copy-start | bytes 18436
  145.3 142.6 %all-to-all-start = ((f32[32,64,768]{2,0,1:T(8,128)}), f32[32,64,768]{2,0,1:T(8,128)}, u32[]{:S(2)}, u32[]{:S(2)}) async-start(f32[32,64,768]{2,0,1:T(8,128)} %copy.57), calls=%async_computation | async-start | bytes 12582912 | tf_op jit(solution)/shard_map/all_to_all | solution.py:144
  193.1 101.2 %slice-start.10 = ((s8[6291456]{0:T(1024)(128)(4,1)}), s8[2097152]{0:T(1024)(128)(4,1)S(1)}, s32[]{:S(2)}) async-start(s8[6291456]{0:T(1024)(128)(4,1)} %bitcast.200), calls=%async_computation.14 | async-start | bytes 4194304
  287.9 6.4 slice-start.11
  291.6 2.7 copy-start.4
  302.2 9.9 copy-start.5
  312.1 13.8 copy-start.1
  312.1 23.6 %slice-start.4 = ((s8[6291456]{0:T(1024)(128)(4,1)}), s8[4194304]{0:T(1024)(128)(4,1)S(1)}, s32[]{:S(2)}) async-start(s8[6291456]{0:T(1024)(128)(4,1)} %bitcast.189), calls=%async_computation.8 | async-start | bytes 8388608
  312.1 23.6 %slice-start.8 = ((s8[6291456]{0:T(1024)(128)(4,1)}), s8[4194304]{0:T(1024)(128)(4,1)S(1)}, s32[]{:S(2)}) async-start(s8[6291456]{0:T(1024)(128)(4,1)} %bitcast.198), calls=%async_computation.12 | async-start | bytes 8388608
  325.9 9.9 slice-start.5
  325.9 9.9 slice-start.9
  353.8 13.2 copy-start.6
  367.0 9.5 copy-start.7
  367.0 19.4 %slice-start = ((s8[8388608]{0:T(1024)(128)(4,1)}), s8[4194304]{0:T(1024)(128)(4,1)S(1)}, s32[]{:S(2)}) async-start(s8[8388608]{0:T(1024)(128)(4,1)} %bitcast.182), calls=%async_computation.4 | async-start | bytes 8388608
  367.0 19.4 %slice-start.6 = ((s8[8388608]{0:T(1024)(128)(4,1)}), s8[4194304]{0:T(1024)(128)(4,1)S(1)}, s32[]{:S(2)}) async-start(s8[8388608]{0:T(1024)(128)(4,1)} %bitcast.192), calls=%async_computation.10 | async-start | bytes 8388608
  376.5 9.9 slice-start.1
  376.5 9.9 slice-start.7
  396.0 14.9 copy-start.2
  421.8 9.6 copy-start.8
  488.4 36.9 %slice-start.2 = ((s8[6291456]{0:T(1024)(128)(4,1)}), s8[2097152]{0:T(1024)(128)(4,1)S(1)}, s32[]{:S(2)}) async-start(s8[6291456]{0:T(1024)(128)(4,1)} %bitcast.184), calls=%async_computation.6 | async-start | bytes 4194304
  488.4 142.3 %all-to-all-start.2 = ((f32[512,4,768]{2,1,0:T(4,128)}), f32[512,4,768]{2,1,0:T(4,128)}, u32[]{:S(2)}, u32[]{:S(2)}) async-start(f32[512,4,768]{2,1,0:T(4,128)} %copy.72), calls=%async_computation.2 | async-start | bytes 12582912 | tf_op jit(solution)/shard_map/all_to_all | solution.py:151
  516.7 8.7 slice-start.3
  630.7 142.6 %all-to-all-start.3 = ((f32[512,4,768]{2,1,0:T(4,128)}), f32[512,4,768]{2,1,0:T(4,128)}, u32[]{:S(2)}, u32[]{:S(2)}) async-start(f32[512,4,768]{2,1,0:T(4,128)} %copy.76), calls=%async_computation.3 | async-start | bytes 12582912 | tf_op jit(solution)/shard_map/all_to_all | solution.py:152
  791.9 15.1 %copy-start.10 = (f32[32,128]{1,0:T(8,128)S(1)}, f32[32,128]{1,0:T(8,128)}, u32[]{:S(2)}) copy-start(f32[32,128]{1,0:T(8,128)} %copy-done.9) | copy-start | bytes 49156
  792.0 15.1 %copy-start.12 = (f32[32,128]{1,0:T(8,128)S(1)}, f32[32,128]{1,0:T(8,128)}, u32[]{:S(2)}) copy-start(f32[32,128]{1,0:T(8,128)} %copy-done.11) | copy-start | bytes 49156
  792.0 15.1 %copy-start.16 = (f32[768]{0:T(1024)S(1)}, f32[768]{0:T(1024)}, u32[]{:S(2)}) copy-start(f32[768]{0:T(1024)} %param.16) | copy-start | bytes 9220
  792.0 15.1 %copy-start.18 = (f32[768]{0:T(1024)S(1)}, f32[768]{0:T(1024)}, u32[]{:S(2)}) copy-start(f32[768]{0:T(1024)} %param.15) | copy-start | bytes 9220
  826.2 4.6 copy-start
  826.2 1.5 copy-start.19
  826.3 1.5 copy-start.20
  827.8 3.0 copy-start.21
  830.8 126.3 %copy-start.22 = (f32[768]{0:T(1024)S(1)}, f32[768]{0:T(1024)}, u32[]{:S(2)}) copy-start(f32[768]{0:T(1024)} %param.26) | copy-start | bytes 9220
